TPU v7x, 128 devices: a whole 4x4x4 slice. The times are simulated.
128 devices in a mesh: view: 8 (over y, z_lo), depth: 16 (over x, z_hi, core).
Axes of the slice: x: 4, y: 4, z: 4 (z_hi: 2, z_lo: 2; z = z_hi * 2 + z_lo), core: 2. Of those that a mesh axis runs over, the one named last changes fastest.
Arguments:
- estimate: float32 [128, 128, 256], P('depth', 'view'), may hold values from 0.5 to 2
- observed: float32 [16, 128, 128, 256], P('view', 'depth'), may hold values from 0.05 to 30, as said below
- voxel_weights: bfloat16 [16, 8, 128, 128, 256], P('view', None, 'depth'), may hold values from 0.029907227 to 0.29882812
- lateral_taps: float32 [16, 8, 2, 9], P('view'), may hold values from 0.05 to 1
- axial_taps: float32 [16, 9], P('view'), may hold values from 0.05 to 1
Outputs:
- updated: float32 [128, 128, 256], P('depth', 'view')
- divergence: float32 [16], P('view')
Inputs may be any that keep to these rules, and one draw needn't show every extreme that they name: `observed`: strictly positive.
All inputs are finite; a program needn't handle non-finite values.
Results may differ from a plain program's by a relative error of at most 0.0003.
Values sent between devices are 32-bit elements; how exact they have to be, the bound alone decides.
A program may use at most 128 MiB of HBM per device.

v0:
```python
import jax
import jax.numpy as jnp
from jax import lax
from jax.sharding import PartitionSpec as P

BASES = 8
TAPS = 9
RADIUS = 4
ITERS = 2


def padded_2(cells, sides, width):
    for axis, dim in sides:
        count = lax.axis_size(axis)
        ends = count - 1
        head = lax.slice_in_dim(cells, 0, width, axis=dim)
        tail = lax.slice_in_dim(cells, cells.shape[dim] - width, cells.shape[dim], axis=dim)
        cells = jnp.concatenate(
            [
                lax.ppermute(tail, axis, [(i, (i + 1) % count) for i in range(ends)]),
                cells,
                lax.ppermute(head, axis, [((i + 1) % count, i) for i in range(ends)]),
            ],
            axis=dim,
        )
    return cells


def lateral_forward(volume, weights, lateral):
    height = volume.shape[1]
    breadth = volume.shape[2]
    padded = jnp.pad(volume, ((0, 0), (RADIUS, RADIUS), (0, 0)))
    stacked = jnp.zeros((BASES,) + volume.shape, jnp.float32)
    for tap_index in range(TAPS):
        stacked = (
            stacked
            + lateral[:, 0, tap_index].reshape(-1, 1, 1, 1)
            * padded[None, :, tap_index : tap_index + height, :]
        )
    padded = jnp.pad(stacked, ((0, 0), (0, 0), (0, 0), (RADIUS, RADIUS)))
    blurred = jnp.zeros(stacked.shape, jnp.float32)
    for tap_index in range(TAPS):
        blurred = (
            blurred
            + lateral[:, 1, tap_index].reshape(-1, 1, 1, 1)
            * padded[:, :, :, tap_index : tap_index + breadth]
        )
    return jnp.sum(weights.astype(jnp.float32) * blurred, axis=0)


def lateral_adjoint(values, weights, lateral):
    height = values.shape[1]
    breadth = values.shape[2]
    stacked = weights.astype(jnp.float32) * values[None]
    padded = jnp.pad(stacked, ((0, 0), (0, 0), (0, 0), (RADIUS, RADIUS)))
    blurred = jnp.zeros(stacked.shape, jnp.float32)
    for tap_index in range(TAPS):
        offset = 2 * RADIUS - tap_index
        blurred = (
            blurred
            + lateral[:, 1, tap_index].reshape(-1, 1, 1, 1)
            * padded[:, :, :, offset : offset + breadth]
        )
    padded = jnp.pad(blurred, ((0, 0), (0, 0), (RADIUS, RADIUS), (0, 0)))
    summed = jnp.zeros(stacked.shape, jnp.float32)
    for tap_index in range(TAPS):
        offset = 2 * RADIUS - tap_index
        summed = (
            summed
            + lateral[:, 0, tap_index].reshape(-1, 1, 1, 1)
            * padded[:, :, offset : offset + height, :]
        )
    return jnp.sum(summed, axis=0)


def body(estimate, observed, voxel_weights, lateral_taps, axial_taps):
    view_count = observed.shape[0]
    planes = observed.shape[1]
    height = observed.shape[2]
    breadth = observed.shape[3]
    lateral_all = lateral_taps / jnp.sum(lateral_taps, axis=-1, keepdims=True)
    axial_all = axial_taps / jnp.sum(axial_taps, axis=-1, keepdims=True)
    views_total = view_count * lax.axis_size("view")
    voxel_total = planes * lax.axis_size("depth") * height * breadth

    def back_project(values):
        fields = jnp.stack(
            [
                lateral_adjoint(
                    values[view_index], voxel_weights[view_index], lateral_all[view_index]
                )
                for view_index in range(view_count)
            ]
        )
        rimmed = padded_2(fields, (("depth", 1),), RADIUS)
        summed = jnp.zeros(fields.shape, jnp.float32)
        for tap_index in range(TAPS):
            offset = 2 * RADIUS - tap_index
            summed = (
                summed
                + axial_all[:, tap_index].reshape(-1, 1, 1, 1) * rimmed[:, offset : offset + planes]
            )
        return summed

    sensitivity = back_project(jnp.ones(observed.shape, jnp.float32))
    current = estimate
    for iteration in range(ITERS):
        gathered = lax.all_gather(current, "view", axis=1, tiled=True)
        extended = padded_2(gathered, (("depth", 0),), RADIUS)
        depth_blur = jnp.zeros(observed.shape, jnp.float32)
        for tap_index in range(TAPS):
            depth_blur = (
                depth_blur
                + axial_all[:, tap_index].reshape(-1, 1, 1, 1)
                * extended[None, tap_index : tap_index + planes]
            )
        predicted = jnp.stack(
            [
                lateral_forward(
                    depth_blur[view_index], voxel_weights[view_index], lateral_all[view_index]
                )
                for view_index in range(view_count)
            ]
        )
        ratios = observed / predicted
        if iteration == ITERS - 1:
            local_sums = jnp.sum(observed * jnp.log(ratios) - observed + predicted, axis=(1, 2, 3))
            divergence = lax.psum(local_sums, "depth") / voxel_total
        log_terms = jnp.sum(jnp.log(back_project(ratios) / sensitivity), axis=0)
        portion = lax.psum_scatter(log_terms, "view", scatter_dimension=1, tiled=True)
        current = current * jnp.exp(portion / views_total)
    return (current, divergence)


def solution(mesh):
    placed = (
        P("depth", "view", None),
        P("view", "depth", None, None),
        P("view", None, "depth", None, None),
        P("view", None, None, None),
        P("view", None),
    )
    return jax.shard_map(
        body,
        mesh=mesh,
        in_specs=placed,
        out_specs=(P("depth", "view", None), P("view")),
        check_vma=False,
    )
```

profile of v0, /device:TPU:0, one launch (start us, length us, event | category | flops | bytes accessed | tf_op | source)
XLA Modules:
  0.0 987.2 jit_solution(13226522171102740828)
XLA Ops:
  7.2 0.7 all-gather.3.cloned.1.call-update
  7.9 0.8 reduce_sum.135
  8.7 0.9 fusion.233
  9.7 11.6 %bitcast_convert_fusion.1 = (f32[8,8,128,256]{3,2,1,0:T(8,128)}, f32[8,8,128,256]{3,2,1,0:T(8,128)}) fusion(bf16[2,8,8,128,256]{4,3,2,1,0:T(8,128)(2,1)} %param.7), kind=kLoop, calls=%fused_computation.313 | loop fusion | flops 4194304 | bytes 25165824 | tf_op jit(solution)/shard_map/convert_element_type | solution.py:54
  21.2 29.8 %all-gather.3.cloned.1.call-done = f32[8,128,256]{2,1,0:T(8,128)} async-done(((f32[8,16,256]{2,1,0:T(8,128)}), f32[8,128,256]{2,1,0:T(8,128)}) %all-gather.3.cloned.1.call-update) | async-done | bytes 1048592 | tf_op jit(solution)/shard_map/all_gather | solution.py:108
  51.1 1.3 fusion.240
  52.4 1.3 collective-permute-start
  53.8 1.3 collective-permute-start.1
  55.9 0.5 slice_reduce_fusion.16
  56.4 1.4 constant_dynamic-update-slice_fusion
  57.8 3.5 collective-permute-done.1
  61.9 0.5 fusion.237
  62.6 1.8 multiply_add_fusion.5
  64.5 3.1 pad_slice_fusion.133
  67.6 7.6 multiply_add_fusion.3
  75.2 78.7 %fusion.5 = (f32[8,8,128,256]{3,2,1,0:T(8,128)}, f32[8,128,256]{2,1,0:T(8,128)}) fusion(f32[8,8,128,256]{3,2,1,0:T(8,128)} %get-tuple-element.59, f32[8]{0:T(128)S(1)} %get-tuple-element.3, f32[8]{0:T(128)S(1)} %get-tuple-element.4, f32[8]{0:T(128)S(1)} %get-tuple-element.5, f32[8]{0:T(128)S(1)} %get-tuple-element.6, f32[8]{0:T(128)S(1)} %get-tuple-element.7, ...), kind=kLoop, calls=%fused_computation.95 | loop fusion | flops 77332480 | bytes 30408992 | tf_op jit(solution)/shard_map/add | solution.py:60
  153.9 9.1 multiply_add_fusion.2
  163.1 85.2 %fusion.12 = (f32[8,8,128,256]{3,2,1,0:T(8,128)}, f32[8,128,256]{2,1,0:T(8,128)}) fusion(f32[8,8,128,256]{3,2,1,0:T(8,128)} %get-tuple-element.60, f32[8]{0:T(128)S(1)} %get-tuple-element.21, f32[8]{0:T(128)S(1)} %get-tuple-element.22, f32[8]{0:T(128)S(1)} %get-tuple-element.23, f32[8]{0:T(128)S(1)} %get-tuple-element.24, f32[8]{0:T(128)S(1)} %get-tuple-element.25, ...), kind=kLoop, calls=%fused_computation.102 | loop fusion | flops 77332480 | bytes 30408992 | tf_op jit(solution)/shard_map/add | solution.py:60
  248.2 1.5 maximum_divide_fusion
  249.9 9.2 convert_multiply_fusion.8
  259.1 42.7 %fusion.70 = f32[8,8,128,256]{3,2,1,0:T(8,128)} fusion(f32[8,8,128,256]{3,2,1,0:T(8,128)} %get-tuple-element.62, f32[8]{0:T(128)S(1)} %get-tuple-element.21, f32[8]{0:T(128)S(1)} %get-tuple-element.22, f32[8]{0:T(128)S(1)} %get-tuple-element.23, f32[8]{0:T(128)S(1)} %get-tuple-element.24, f32[8]{0:T(128)S(1)} %get-tuple-element.25, ...), kind=kLoop, calls=%fused_computation.160 | loop fusion | flops 35651584 | bytes 16777504 | tf_op jit(solution)/shard_map/add | solution.py:60
  301.8 42.1 %fusion.54 = f32[8,8,128,256]{3,2,1,0:T(8,128)} fusion(f32[8,8,128,256]{3,2,1,0:T(8,128)} %get-tuple-element.61, f32[8]{0:T(128)S(1)} %get-tuple-element.3, f32[8]{0:T(128)S(1)} %get-tuple-element.4, f32[8]{0:T(128)S(1)} %get-tuple-element.5, f32[8]{0:T(128)S(1)} %get-tuple-element.6, f32[8]{0:T(128)S(1)} %get-tuple-element.7, f32[8]{0:T(128)S(1)} %get-tuple-element.8, ...), kind=kLoop, calls=%fused_computation.144 | loop fusion | flops 35651584 | bytes 16777504 | tf_op jit(solution)/shard_map/add | solution.py:60
  343.8 70.9 %add_reduce_fusion.4 = (f32[8,128,256]{2,1,0:T(8,128)S(1)}, f32[8,128,256]{2,1,0:T(8,128)}) fusion(f32[8,8,128,256]{3,2,1,0:T(8,128)} %fusion.70, f32[8]{0:T(128)S(1)} %get-tuple-element.29, f32[8]{0:T(128)S(1)} %get-tuple-element.30, f32[8]{0:T(128)S(1)} %get-tuple-element.31, f32[8]{0:T(128)S(1)} %get-tuple-element.32, f32[8]{0:T(128)S(1)} %get-tuple-element.33, ...), kind=kLoop, calls=%fused_computation.292 | loop fusion | flops 74973184 | bytes 18874656 | tf_op jit(solution)/shard_map/reduce_sum | solution.py:73
  414.7 47.9 %add_reduce_fusion.5 = (f32[8,128,256]{2,1,0:T(8,128)}, f32[8,128,256]{2,1,0:T(8,128)}) fusion(f32[8,8,128,256]{3,2,1,0:T(8,128)S(1)} %copy-done, f32[8]{0:T(128)S(1)} %get-tuple-element.11, f32[8]{0:T(128)S(1)} %get-tuple-element.12, f32[8]{0:T(128)S(1)} %get-tuple-element.13, f32[8]{0:T(128)S(1)} %get-tuple-element.14, f32[8]{0:T(128)S(1)} %get-tuple-element.15, ...), kind=kLoop, calls=%fused_computation.301 | loop fusion | flops 74973184 | bytes 18874656 | tf_op jit(solution)/shard_map/reduce_sum | solution.py:73
  462.6 1.9 fusion.228
  464.4 1.4 collective-permute-start.4
  465.9 12.4 %collective-permute-start.5 = (f32[2,4,128,256]{3,2,1,0:T(8,128)S(1)}, f32[2,4,128,256]{3,2,1,0:T(8,128)S(1)}, u32[]{:S(2)}, u32[]{:S(2)}) collective-permute-start(f32[2,4,128,256]{3,2,1,0:T(8,128)S(1)} %get-tuple-element.76), channel_id=1, source_target_pairs={{0,1},{1,2},{2,3},{3,4},{4,5},{5,6},{6,7},{7,8},{8,9},{9,10},{10,1... | collective-permute-start | bytes 3145736 | tf_op jit(solution)/shard_map/ppermute | solution.py:20
  478.3 1.4 fusion.230
  479.7 1.3 collective-permute-start.2
  481.0 6.7 collective-permute-start.3
  487.7 0.7 pad_maximum_fusion.1
  488.5 1.2 collective-permute-done.3
  489.7 0.7 pad_maximum_fusion
  490.5 8.2 log_reduce_fusion.1
  498.8 74.6 %reduce-scatter.3.cloned.1.call-done = f32[8,16,256]{2,1,0:T(8,128)} async-done(((f32[8,128,256]{2,1,0:T(8,128)}), f32[8,16,256]{2,1,0:T(8,128)}) %reduce-scatter.3.cloned.1.call-update) | async-done | bytes 131088 | tf_op jit(solution)/shard_map/reduce_scatter | solution.py:130
  573.4 1.6 exponential_multiply_fusion.1
  575.1 38.2 %all-gather.5.cloned.1.call-done = f32[8,128,256]{2,1,0:T(8,128)} async-done(((f32[8,16,256]{2,1,0:T(8,128)}), f32[8,128,256]{2,1,0:T(8,128)}) %all-gather.5.cloned.1.call-update) | async-done | bytes 1048592 | tf_op jit(solution)/shard_map/all_gather | solution.py:108
  613.2 1.3 fusion.239
  614.5 1.3 collective-permute-start.6
  615.9 1.3 collective-permute-start.7
  617.4 1.4 constant_dynamic-update-slice_fusion.4
  618.8 4.6 collective-permute-done.7
  624.7 1.3 multiply_add_fusion.4
  626.2 1.0 pad_slice_fusion.125
  627.2 7.6 multiply_add_fusion.1
  634.8 41.3 %fusion.6 = f32[8,128,256]{2,1,0:T(8,128)S(1)} fusion(f32[8,8,128,256]{3,2,1,0:T(8,128)} %multiply_add_fusion.1, f32[8]{0:T(128)S(1)} %get-tuple-element.3, f32[8]{0:T(128)S(1)} %get-tuple-element.4, f32[8]{0:T(128)S(1)} %get-tuple-element.5, f32[8]{0:T(128)S(1)} %get-tuple-element.6, f32[8]{0:T(128)S(1)} %get-tuple-element.7, f32[8]{0:T(128)S(1)} %get-tuple-element.8, ...), kind=kLoop, calls=%fused_computation.96 | loop fusion | flops 41680896 | bytes 13631776 | tf_op jit(solution)/shard_map/reduce_sum | solution.py:48
  676.1 1.0 pad_slice_fusion.117
  677.1 7.5 multiply_add_fusion
  684.6 42.8 %fusion.13 = f32[8,128,256]{2,1,0:T(8,128)} fusion(f32[8,8,128,256]{3,2,1,0:T(8,128)} %multiply_add_fusion, f32[8]{0:T(128)S(1)} %get-tuple-element.21, f32[8]{0:T(128)S(1)} %get-tuple-element.22, f32[8]{0:T(128)S(1)} %get-tuple-element.23, f32[8]{0:T(128)S(1)} %get-tuple-element.24, f32[8]{0:T(128)S(1)} %get-tuple-element.25, f32[8]{0:T(128)S(1)} %get-tuple-element.26, ...), kind=kLoop, calls=%fused_computation.103 | loop fusion | flops 41680896 | bytes 13631776 | tf_op jit(solution)/shard_map/reduce_sum | solution.py:48
  727.4 2.0 fusion.215
  729.6 9.2 convert_multiply_fusion.5
  738.7 42.7 %fusion.156 = f32[8,8,128,256]{3,2,1,0:T(8,128)} fusion(f32[8,8,128,256]{3,2,1,0:T(8,128)} %get-tuple-element.58, f32[8]{0:T(128)S(1)} %get-tuple-element.21, f32[8]{0:T(128)S(1)} %get-tuple-element.22, f32[8]{0:T(128)S(1)} %get-tuple-element.23, f32[8]{0:T(128)S(1)} %get-tuple-element.24, f32[8]{0:T(128)S(1)} %get-tuple-element.25, ...), kind=kLoop, calls=%fused_computation.246 | loop fusion | flops 35651584 | bytes 16777504 | tf_op jit(solution)/shard_map/add | solution.py:60
  781.4 36.7 %add_reduce_fusion = f32[8,128,256]{2,1,0:T(8,128)S(1)} fusion(f32[8,8,128,256]{3,2,1,0:T(8,128)} %fusion.156, f32[8]{0:T(128)S(1)} %get-tuple-element.29, f32[8]{0:T(128)S(1)} %get-tuple-element.30, f32[8]{0:T(128)S(1)} %get-tuple-element.31, f32[8]{0:T(128)S(1)} %get-tuple-element.32, f32[8]{0:T(128)S(1)} %get-tuple-element.33, ...), kind=kLoop, calls=%fused_computation.254 | loop fusion | flops 37486592 | bytes 9437472 | tf_op jit(solution)/shard_map/reduce_sum | solution.py:73
  818.1 42.0 %fusion.140 = f32[8,8,128,256]{3,2,1,0:T(8,128)} fusion(f32[8,8,128,256]{3,2,1,0:T(8,128)} %get-tuple-element.57, f32[8]{0:T(128)S(1)} %get-tuple-element.3, f32[8]{0:T(128)S(1)} %get-tuple-element.4, f32[8]{0:T(128)S(1)} %get-tuple-element.5, f32[8]{0:T(128)S(1)} %get-tuple-element.6, f32[8]{0:T(128)S(1)} %get-tuple-element.7, f32[8]{0:T(128)S(1)} %get-tuple-element.8, ...), kind=kLoop, calls=%fused_computation.230 | loop fusion | flops 35651584 | bytes 16777504 | tf_op jit(solution)/shard_map/add | solution.py:60
  860.1 36.6 %add_reduce_fusion.1 = f32[8,128,256]{2,1,0:T(8,128)S(1)} fusion(f32[8,8,128,256]{3,2,1,0:T(8,128)} %fusion.140, f32[8]{0:T(128)S(1)} %get-tuple-element.11, f32[8]{0:T(128)S(1)} %get-tuple-element.12, f32[8]{0:T(128)S(1)} %get-tuple-element.13, f32[8]{0:T(128)S(1)} %get-tuple-element.14, f32[8]{0:T(128)S(1)} %get-tuple-element.15, ...), kind=kLoop, calls=%fused_computation.263 | loop fusion | flops 37486592 | bytes 9437472 | tf_op jit(solution)/shard_map/reduce_sum | solution.py:73
  896.9 1.4 collective-permute-start.8
  898.3 12.5 %collective-permute-start.9 = (f32[2,4,128,256]{3,2,1,0:T(8,128)S(1)}, f32[2,4,128,256]{3,2,1,0:T(8,128)S(1)}, u32[]{:S(2)}, u32[]{:S(2)}) collective-permute-start(f32[2,4,128,256]{3,2,1,0:T(8,128)S(1)} %get-tuple-element.68), channel_id=1, source_target_pairs={{0,1},{1,2},{2,3},{3,4},{4,5},{5,6},{6,7},{7,8},{8,9},{9,10},{10,1... | collective-permute-start | bytes 3145736 | tf_op jit(solution)/shard_map/ppermute | solution.py:20
  911.0 2.1 collective-permute-done.9
  913.0 0.8 pad_maximum_fusion.2
  913.9 3.6 log_reduce_fusion
  917.5 55.2 %psum.7 = f32[2]{0:T(128)S(1)} all-reduce(f32[2]{0:T(128)S(1)} %get-tuple-element.63), channel_id=1, replica_groups=mesh['view'=8,'depth'=16] {'depth'}, use_global_device_ids=true, to_apply=%region_17.18 | all-reduce | flops 2 | bytes 16 | tf_op jit(solution)/shard_map/psum | solution.py:128
  972.7 0.5 broadcast_multiply_fusion
  973.2 5.7 reduce-scatter.5.cloned.1.call-done
  978.9 1.6 exponential_multiply_fusion
  (55 shorter events, 4.3 us)
Async XLA Ops:
  7.2 43.9 %all-gather.3.cloned.1.call-start = ((), (), s32[]{:S(2)}) async-start(), calls=%async_computation.2 | async-start | bytes 1179648 | tf_op jit(solution)/shard_map/all_gather | solution.py:108
  7.9 565.5 %reduce-scatter.3.cloned.1.call-start = ((), (), s32[]{:S(2)}) async-start(), calls=%async_computation.3 | async-start | bytes 1179648 | tf_op jit(solution)/shard_map/reduce_scatter | solution.py:130
  9.7 44.1 %copy-start.12 = (f32[2,9]{1,0:T(2,128)S(1)}, f32[2,9]{1,0:T(2,128)}, u32[]{:S(2)}) copy-start(f32[2,9]{1,0:T(2,128)} %param.9) | copy-start | bytes 220
  52.4 4.0 collective-permute-start
  53.8 7.5 collective-permute-start.1
  61.4 1.2 copy-start.4
  163.0 85.2 %copy-start.6 = (f32[2,8,128,256]{3,2,1,0:T(8,128)S(1)}, f32[2,8,128,256]{3,2,1,0:T(8,128)}, u32[]{:S(2)}) copy-start(f32[2,8,128,256]{3,2,1,0:T(8,128)} %param.6) | copy-start | bytes 6291460
  163.0 85.2 %copy-start.9 = (f32[8,128,256]{2,1,0:T(8,128)S(1)}, f32[8,128,256]{2,1,0:T(8,128)}, u32[]{:S(2)}) copy-start(f32[8,128,256]{2,1,0:T(8,128)} %get-tuple-element.54) | copy-start | bytes 3145732
  343.8 70.9 %copy-start = (f32[8,8,128,256]{3,2,1,0:T(8,128)S(1)}, f32[8,8,128,256]{3,2,1,0:T(8,128)}, u32[]{:S(2)}) copy-start(f32[8,8,128,256]{3,2,1,0:T(8,128)} %fusion.54) | copy-start | bytes 25165828
  462.6 25.2 %copy-start.1 = (f32[8,128,256]{2,1,0:T(8,128)S(1)}, f32[8,128,256]{2,1,0:T(8,128)}, u32[]{:S(2)}) copy-start(f32[8,128,256]{2,1,0:T(8,128)} %get-tuple-element.41) | copy-start | bytes 3145732
  462.6 25.2 %copy-start.3 = (f32[8,128,256]{2,1,0:T(8,128)S(1)}, f32[8,128,256]{2,1,0:T(8,128)}, u32[]{:S(2)}) copy-start(f32[8,128,256]{2,1,0:T(8,128)} %get-tuple-element.39) | copy-start | bytes 3145732
  464.4 25.3 %copy-start.2 = (f32[8,128,256]{2,1,0:T(8,128)S(1)}, f32[8,128,256]{2,1,0:T(8,128)}, u32[]{:S(2)}) copy-start(f32[8,128,256]{2,1,0:T(8,128)} %get-tuple-element.38) | copy-start | bytes 3145732
  464.4 23.3 %collective-permute-start.4 = (f32[2,4,128,256]{3,2,1,0:T(8,128)S(1)}, f32[2,4,128,256]{3,2,1,0:T(8,128)S(1)}, u32[]{:S(2)}, u32[]{:S(2)}) collective-permute-start(f32[2,4,128,256]{3,2,1,0:T(8,128)S(1)} %get-tuple-element.75), channel_id=1, source_target_pairs={{1,0},{2,1},{3,2},{4,3},{5,4},{6,5},{7,6},{8,7},{9,8},{10,9},{11,1... | collective-permute-start | bytes 3145736 | tf_op jit(solution)/shard_map/ppermute | solution.py:22
  465.9 21.8 %collective-permute-start.5 = (f32[2,4,128,256]{3,2,1,0:T(8,128)S(1)}, f32[2,4,128,256]{3,2,1,0:T(8,128)S(1)}, u32[]{:S(2)}, u32[]{:S(2)}) collective-permute-start(f32[2,4,128,256]{3,2,1,0:T(8,128)S(1)} %get-tuple-element.76), channel_id=1, source_target_pairs={{0,1},{1,2},{2,3},{3,4},{4,5},{5,6},{6,7},{7,8},{8,9},{9,10},{10,1... | collective-permute-start | bytes 3145736 | tf_op jit(solution)/shard_map/ppermute | solution.py:20
  479.7 8.8 collective-permute-start.2
  481.0 8.7 collective-permute-start.3
  490.5 82.9 %copy-start.11 = (f32[8,16,256]{2,1,0:T(8,128)S(1)}, f32[8,16,256]{2,1,0:T(8,128)}, u32[]{:S(2)}) copy-start(f32[8,16,256]{2,1,0:T(8,128)} %param.5) | copy-start | bytes 393220
  498.7 114.5 %all-gather.5.cloned.1.call-start = ((), (), s32[]{:S(2)}) async-start(), calls=%async_computation.4 | async-start | bytes 1179648 | tf_op jit(solution)/shard_map/all_gather | solution.py:108
  575.0 403.9 %reduce-scatter.5.cloned.1.call-start = ((), (), s32[]{:S(2)}) async-start(), calls=%async_computation.5 | async-start | bytes 1179648 | tf_op jit(solution)/shard_map/reduce_scatter | solution.py:130
  614.5 2.8 collective-permute-start.6
  615.9 7.6 collective-permute-start.7
  623.5 1.2 copy-start.5
  684.6 42.8 %copy-start.7 = (f32[2,8,128,256]{3,2,1,0:T(8,128)S(1)}, f32[2,8,128,256]{3,2,1,0:T(8,128)}, u32[]{:S(2)}) copy-start(f32[2,8,128,256]{3,2,1,0:T(8,128)} %param.6) | copy-start | bytes 6291460
  896.7 17.2 %copy-start.8 = (f32[2,8,128,256]{3,2,1,0:T(8,128)S(1)}, f32[2,8,128,256]{3,2,1,0:T(8,128)}, u32[]{:S(2)}) copy-start(f32[2,8,128,256]{3,2,1,0:T(8,128)} %get-tuple-element.52) | copy-start | bytes 6291460
  896.9 14.1 %collective-permute-start.8 = (f32[2,4,128,256]{3,2,1,0:T(8,128)S(1)}, f32[2,4,128,256]{3,2,1,0:T(8,128)S(1)}, u32[]{:S(2)}, u32[]{:S(2)}) collective-permute-start(f32[2,4,128,256]{3,2,1,0:T(8,128)S(1)} %get-tuple-element.67), channel_id=1, source_target_pairs={{1,0},{2,1},{3,2},{4,3},{5,4},{6,5},{7,6},{8,7},{9,8},{10,9},{11,1... | collective-permute-start | bytes 3145736 | tf_op jit(solution)/shard_map/ppermute | solution.py:22
  898.3 14.7 %collective-permute-start.9 = (f32[2,4,128,256]{3,2,1,0:T(8,128)S(1)}, f32[2,4,128,256]{3,2,1,0:T(8,128)S(1)}, u32[]{:S(2)}, u32[]{:S(2)}) collective-permute-start(f32[2,4,128,256]{3,2,1,0:T(8,128)S(1)} %get-tuple-element.68), channel_id=1, source_target_pairs={{0,1},{1,2},{2,3},{3,4},{4,5},{5,6},{6,7},{7,8},{8,9},{9,10},{10,1... | collective-permute-start | bytes 3145736 | tf_op jit(solution)/shard_map/ppermute | solution.py:20
  913.9 65.1 %copy-start.10 = (f32[8,16,256]{2,1,0:T(8,128)S(1)}, f32[8,16,256]{2,1,0:T(8,128)}, u32[]{:S(2)}) copy-start(f32[8,16,256]{2,1,0:T(8,128)} %exponential_multiply_fusion.1) | copy-start | bytes 393220
Sparse Core Ops, SparseCore 0:
  9.6 41.4 all-gather.2
  498.8 74.5 reduce-scatter.2
  575.6 37.5 all-gather.4
  917.6 61.2 reduce-scatter.4
where the time goes:
time: 991 us; the launch traced here: 987 us
  other arithmetic  701 us (71%)
  waiting for transfers between devices  161 us (16%)
  blocking collectives  55.2 us (6%)
  starting transfers between devices  41.1 us (4%)
  local copies, waits for them, and re-layouts  14.9 us (2%)
  between operations  14.4 us (1%)
    add x6, other arithmetic, lateral_adjoint(): blurred + lateral[:, 1, tap_index].reshape(-1, 1, 1, 1) * padded[:, :, :,...  333 us
    reduce_sum x4, other arithmetic, lateral_adjoint(): return jnp.sum(summed, axis=0)  192 us
    reduce_sum x2, other arithmetic, lateral_forward(): return jnp.sum(weights.astype(jnp.float32) * blurred, axis=0)  84.1 us
    reduce_scatter x2, waiting for transfers between devices, body(): lax.psum_scatter(log_terms, 'view', scatter_dimension=1, tiled=True)  80.4 us
    all_gather x2, waiting for transfers between devices, body(): gathered = lax.all_gather(current, 'view', axis=1, tiled=True)  68 us
    psum x1, blocking collectives, body(): divergence = lax.psum(local_sums, 'depth') / voxel_total  55.2 us
    ppermute x5, starting transfers between devices, padded_2(): lax.ppermute(tail, axis, [(i, (i + 1) % count) for i in range(ends)])  34.3 us
    add x4, other arithmetic, lateral_forward(): stacked + lateral[:, 0, tap_index].reshape(-1, 1, 1, 1) * padded[None, :,...  31.8 us
  transfers between devices with their start and end apart: 14, of which 10 were waited for; matrix products, arithmetic and copies ran while one was open for 2% of the time, Pallas kernels for 0%

commit v1 on v0

v1 whole, which is shorter than its diff:
```python
import numpy as np
import jax
import jax.numpy as jnp
from jax import lax
from jax.experimental import pallas as pl
from jax.experimental.pallas import tpu as pltpu
from jax.sharding import PartitionSpec as P

BASES = 8
TAPS = 9
RADIUS = 4
ITERS = 2
F32 = jnp.float32
BF16 = jnp.bfloat16
ROWS = 16
CHUNK = 32


def spread(count, stride, reach):
    return 1.0 + reach * np.mod(stride * np.arange(count) + 0.13, 1.0)


def scale_tiles():
    rows = np.broadcast_to(spread(8, 0.5698402910, 0.37)[:, None], (8, 256))
    lanes = np.broadcast_to(spread(256, 0.7548776662, 0.41)[None, :], (8, 256))
    return np.stack([rows, 1.0 / rows, lanes, 1.0 / lanes, lanes / rows]).astype(np.float32)


def kernel(
    est, obs, wgt, base_x, base_y, scale, axial, step, tiles,
    out, div_out,
    w, ob, tyf, tya, txf, txa, g, mid, field, s_field, r_field, acc, ratio, log_s, log_r, far, near,
    zbuf, sums, peers,
    load_sem, ag_send, ag_recv, halo_send, halo_recv, rs_send, rs_recv, div_send, div_recv,
):
    vi = lax.axis_index("view")
    d = lax.axis_index("depth")
    y = vi // 2
    zl = vi % 2
    core = d % 2
    v_up = ((y + 1) % 4) * 2 + zl
    v_dn = ((y + 3) % 4) * 2 + zl
    v_z = vi + 1 - 2 * zl
    d_up = (d + 1) % 16
    d_dn = (d + 15) % 16
    d_out = (d + 15 + 2 * core) % 16
    d_in = d + 1 - 2 * core
    partners = [d + 1 - 2 * (d % 2), d + 2 - 4 * ((d // 2) % 2), d + 4 - 8 * ((d // 4) % 2), d + 8 - 16 * (d // 8)]

    loads = [
        pltpu.make_async_copy(est, field.at[pl.ds(4, 8), pl.ds(pl.multiple_of(vi * ROWS, ROWS), ROWS)], load_sem.at[0]),
        pltpu.make_async_copy(wgt.at[0], w.at[0], load_sem.at[1]),
        pltpu.make_async_copy(wgt.at[1], w.at[1], load_sem.at[2]),
        pltpu.make_async_copy(obs, ob, load_sem.at[3]),
    ]
    for copy in loads:
        copy.start()

    barrier = pltpu.get_barrier_semaphore()
    greeted = [
        {"view": v_up}, {"view": v_dn}, {"view": v_z}, {"depth": d_up}, {"depth": d_dn},
        {"depth": partners[1]}, {"depth": partners[2]}, {"depth": partners[3]},
    ]
    for who in greeted:
        pl.semaphore_signal(barrier, inc=1, device_id=who, device_id_type=pl.DeviceIdType.MESH)
    pl.semaphore_wait(barrier, len(greeted))

    def remote(src, dst, send, recv, who):
        return pltpu.make_async_remote_copy(
            src_ref=src, dst_ref=dst, send_sem=send, recv_sem=recv,
            device_id=who, device_id_type=pl.DeviceIdType.MESH,
        )

    def block(first, count, owner):
        return field.at[pl.ds(first, count), pl.ds(pl.multiple_of(owner * ROWS, ROWS), ROWS)]

    def gather(it, part):
        first, count = ((4, 8), (12 * core, 4))[part]
        base = part * 7

        def hop(slot, owner, who):
            ref = block(first, count, owner)
            return remote(ref, ref, ag_send.at[it, base + slot], ag_recv.at[it, base + slot], who)

        mate = v_z
        return [
            hop(0, vi, {"view": v_z}),
            hop(1, vi, {"view": v_up}),
            hop(2, vi, {"view": v_dn}),
            hop(3, mate, {"view": v_up}),
            hop(4, mate, {"view": v_dn}),
            hop(5, v_dn, {"view": v_up}),
            hop(6, v_up + 1 - 2 * zl, {"view": v_dn}),
        ]

    def outer(it):
        return remote(
            block(4 + 4 * core, 4, vi), block(12 - 12 * core, 4, vi),
            ag_send.at[it, 14], ag_recv.at[it, 14], {"depth": d_out},
        )

    def inner(it):
        return remote(
            field.at[pl.ds(8 - 4 * core, 4)], field.at[pl.ds(12 * core, 4)],
            ag_send.at[it, 15], ag_recv.at[it, 15], {"depth": d_in},
        )

    def gather_first(it):
        outer(it).start()
        hops = gather(it, 0)
        for slot in (1, 2, 0):
            hops[slot].start()
        outer(it).wait_recv()
        hops = gather(it, 1)
        for slot in (1, 2, 0):
            hops[slot].start()

    def gather_second(it):
        for part in (0, 1):
            hops = gather(it, part)
            hops[0].wait_recv()
            hops[3].start()
            hops[4].start()
            hops[1].wait_recv()
            hops[5].start()

    def gather_third(it):
        for part in (0, 1):
            hops = gather(it, part)
            hops[4].wait_recv()
            hops[6].start()

    def gather_last(it):
        hops = gather(it, 0)
        for slot in (2, 3, 5, 6):
            hops[slot].wait_recv()
        inner(it).start()
        hops = gather(it, 1)
        for slot in (2, 3, 5, 6):
            hops[slot].wait_recv()
        inner(it).wait_recv()
        for part in (0, 1):
            for hop in gather(it, part):
                hop.wait_send()
        outer(it).wait_send()
        inner(it).wait_send()

        @pl.when(d == 0)
        def _():
            field[pl.ds(0, 4)] = jnp.zeros((4, 128, 256), F32)

        @pl.when(d == 15)
        def _():
            field[pl.ds(12, 4)] = jnp.zeros((4, 128, 256), F32)

    order = [(y + 2) % 4, (y + 1) % 4, (y + 3) % 4, y]

    def halo(buf, turn, v, c, up):
        rows = pl.ds(pl.multiple_of(order[c] * CHUNK, CHUNK), CHUNK)
        source, target = (8, 0) if up else (4, 12)
        slot = (v * 4 + c) * 2 + up
        return remote(
            buf.at[v, pl.ds(source, 4), rows], buf.at[v, pl.ds(target, 4), rows],
            halo_send.at[turn, slot], halo_recv.at[turn, slot], {"depth": d_up if up else d_dn},
        )

    def send_halos(buf, turn, v):
        for c in range(4):
            halo(buf, turn, v, c, 0).start()
            halo(buf, turn, v, c, 1).start()

    def wait_halo_chunk(buf, turn, c):
        for v in (0, 1):
            for up in (0, 1):
                halo(buf, turn, v, c, up).wait_recv()
        rows = pl.ds(pl.multiple_of(order[c] * CHUNK, CHUNK), CHUNK)

        @pl.when(d == 0)
        def _():
            buf[:, pl.ds(0, 4), rows] = jnp.zeros((2, 4, CHUNK, 256), F32)

        @pl.when(d == 15)
        def _():
            buf[:, pl.ds(12, 4), rows] = jnp.zeros((2, 4, CHUNK, 256), F32)

    def wait_halo_sends(buf, turn):
        for v in (0, 1):
            for c in range(4):
                for up in (0, 1):
                    halo(buf, turn, v, c, up).wait_send()

    def rs_hops(it):
        far_rows = order[0] * CHUNK
        up_rows = order[1] * CHUNK
        dn_rows = order[2] * CHUNK
        mate_rows = v_z * ROWS

        def cut(start, count):
            return log_r.at[:, pl.ds(pl.multiple_of(start, ROWS), count)]

        def hop(slot, src, dst, who):
            return remote(src, dst, rs_send.at[it, slot], rs_recv.at[it, slot], who)

        return [
            hop(0, cut(far_rows, ROWS), far.at[0], {"view": v_up}),
            hop(1, cut(far_rows + ROWS, ROWS), far.at[1], {"view": v_dn}),
            hop(2, cut(up_rows, CHUNK), near.at[0], {"view": v_up}),
            hop(3, cut(dn_rows, CHUNK), near.at[1], {"view": v_dn}),
            hop(4, cut(mate_rows, ROWS), zbuf, {"view": v_z}),
        ]

    def build(i, carry):
        v = i // 8
        b = i % 8

        def band(row, size):
            wide = jnp.broadcast_to(row, (size, size))
            turned = pltpu.roll(wide, 0, 1, stride=1, stride_axis=0)
            diff = lax.broadcasted_iota(jnp.int32, (size, size), 1) - lax.broadcasted_iota(jnp.int32, (size, size), 0)
            return jnp.where((diff <= 4) & (diff >= -4), turned, 0.0).astype(BF16)

        txf[i] = band(base_x[i, 1:2], 256)
        txa[i] = band(base_x[i, 0:1], 256)
        fwd = band(base_y[i, 0:1], 128)
        rows = pl.ds(pl.multiple_of(b * 128, 128), 128)
        tyf[v, rows, pl.ds(0, 128)] = fwd
        tyf[v, rows, pl.ds(128, 128)] = fwd
        tya[v, :, rows] = band(base_y[i, 1:2], 128)
        return carry

    def tiled(x, tile):
        return (x.reshape(x.shape[0] // 8, 8, 256) * tile[None]).reshape(x.shape)

    def adjoint(v, values, buf):
        def over_bases(b, carry):
            gain = scale[v * 8 + b]
            for q in range(4):
                weights = w[v, b, pl.ds(2 * q, 2)].reshape(256, 256)
                if values is not None:
                    weights = (weights.astype(F32) * values[pl.ds(2 * q, 2)].reshape(256, 256)).astype(BF16)
                o = jnp.dot(weights, txa[v * 8 + b], preferred_element_type=F32)
                for h in (0, 1):
                    z = 2 * q + h
                    if values is None:
                        tile = tiles[2] * (gain * step[0, v * 8 + z])
                    else:
                        tile = tiles[4] * gain
                    mid[z, b] = tiled(o[h * 128 : h * 128 + 128], tile).astype(BF16)
            return carry

        lax.fori_loop(0, 8, over_bases, 0)

        def over_planes(z, carry):
            o = jnp.dot(tya[v], mid[z].reshape(1024, 256), preferred_element_type=F32)
            buf[v, 4 + z] = tiled(o, tiles[3] * step[1, v * 8 + z])
            return carry

        lax.fori_loop(0, 8, over_planes, 0)

    def forward(v, last):
        def blur(z, carry):
            total = axial[v, 0] * field[z]
            for k in range(1, TAPS):
                total = total + axial[v, k] * field[z + k]
            high = total.astype(BF16)
            g[z, pl.ds(0, 128)] = high
            g[z, pl.ds(128, 128)] = (total - high.astype(F32)).astype(BF16)
            for q in range(4):
                o = jnp.dot(tyf[v, pl.ds(q * 256, 256)], g[z], preferred_element_type=F32)
                for h in (0, 1):
                    b = 2 * q + h
                    tile = tiles[0] * (scale[v * 8 + b] * step[0, v * 8 + z])
                    mid[b, z] = tiled(o[h * 128 : h * 128 + 128], tile).astype(BF16)
            return carry

        lax.fori_loop(0, 8, blur, 0)
        acc[...] = jnp.zeros_like(acc)

        def over_bases(b, carry):
            for q in range(4):
                o = jnp.dot(mid[b, pl.ds(2 * q, 2)].reshape(256, 256), txf[v * 8 + b], preferred_element_type=F32)
                acc[pl.ds(2 * q, 2)] += o.reshape(2, 128, 256) * w[v, b, pl.ds(2 * q, 2)].astype(F32)
            return carry

        lax.fori_loop(0, 8, over_bases, 0)
        if last:
            sums[v] = jnp.zeros((8, 256), F32)

        def quotient(z, carry):
            predicted = tiled(acc[z], tiles[1] * step[1, v * 8 + z])
            seen = ob[v, z]
            fraction = seen / predicted
            ratio[z] = tiled(fraction, tiles[0] * step[0, v * 8 + z])
            if last:
                terms = seen * jnp.log(fraction) - seen + predicted
                sums[v] += jnp.sum(terms.reshape(16, 8, 256), axis=0)
            return carry

        lax.fori_loop(0, 8, quotient, 0)

    def product(buf, rows, z):
        totals = []
        for v in (0, 1):
            total = axial[v, 0] * buf[v, z + 8, rows]
            for k in range(1, TAPS):
                total = total + axial[v, k] * buf[v, z + 8 - k, rows]
            totals.append(total)
        return jnp.log(totals[0] * totals[1])

    def corrections(it, c):
        rows = pl.ds(pl.multiple_of(order[c] * CHUNK, CHUNK), CHUNK)

        def each(z, carry):
            log_r[z, rows] = product(r_field, rows, z) - log_s[z, rows]
            return carry

        lax.fori_loop(0, 8, each, 0)

    def sensitivity_chunk(c):
        wait_halo_chunk(s_field, 0, c)
        rows = pl.ds(pl.multiple_of(order[c] * CHUNK, CHUNK), CHUNK)

        def each(z, carry):
            log_s[z, rows] = product(s_field, rows, z)
            return carry

        lax.fori_loop(0, 8, each, 0)

    def add_rows(start, count, ref):
        rows = pl.ds(pl.multiple_of(start, ROWS), count)
        log_r[:, rows] += ref[...]

    def reduce_chunks(it):
        hops = rs_hops(it)
        for c in range(4):
            if it == 0:
                sensitivity_chunk(c)
            wait_halo_chunk(r_field, 1 + it, c)
            corrections(it, c)
            if c == 0:
                hops[0].start()
                hops[1].start()
            if c == 1:
                hops[0].wait_recv()
                add_rows(order[1] * CHUNK, ROWS, far.at[0])
                hops[2].start()
            if c == 2:
                hops[1].wait_recv()
                add_rows(order[2] * CHUNK + ROWS, ROWS, far.at[1])
                hops[3].start()
        hops[2].wait_recv()
        add_rows(y * CHUNK, CHUNK, near.at[0])
        hops[3].wait_recv()
        add_rows(y * CHUNK, CHUNK, near.at[1])
        hops[4].start()
        hops[4].wait_recv()
        for hop in hops:
            hop.wait_send()
        wait_halo_sends(r_field, 1 + it)
        if it == 0:
            wait_halo_sends(s_field, 0)
        rows = pl.ds(pl.multiple_of(vi * ROWS, ROWS), ROWS)
        log_total = log_r[:, rows] + zbuf[...]
        return rows, field[pl.ds(4, 8), rows] * jnp.exp(log_total * (1.0 / 16.0))

    loads[0].wait()
    gather_first(0)
    lax.fori_loop(0, 16, build, 0)
    loads[1].wait()
    loads[2].wait()
    gather_second(0)
    adjoint(0, None, s_field)
    send_halos(s_field, 0, 0)
    gather_third(0)
    adjoint(1, None, s_field)
    send_halos(s_field, 0, 1)
    loads[3].wait()
    gather_last(0)
    for it in range(ITERS):
        last = it == ITERS - 1
        for v in (0, 1):
            forward(v, last)
            adjoint(v, ratio, r_field)
            send_halos(r_field, 1 + it, v)
        if last:
            for step in range(4):
                copy = remote(sums, peers.at[step], div_send.at[step], div_recv.at[step], {"depth": partners[step]})
                copy.start()
                copy.wait()
                sums[...] += peers[step]
        rows, updated = reduce_chunks(it)
        if last:
            out[...] = updated
        else:
            field[pl.ds(4, 8), rows] = updated
            gather_first(1)
            gather_second(1)
            gather_third(1)
            gather_last(1)
    for v in (0, 1):
        div_out[pl.ds(v, 1)] = jnp.broadcast_to(jnp.sum(sums[v], keepdims=True), (1, 128))


def body(estimate, observed, voxel_weights, lateral_taps, axial_taps):
    planes = observed.shape[1]
    voxel_total = planes * lax.axis_size("depth") * observed.shape[2] * observed.shape[3]
    axial = axial_taps / jnp.sum(axial_taps, axis=-1, keepdims=True)
    coarse = lax.reduce_precision(lateral_taps, 8, 7)
    totals = jnp.sum(coarse, axis=-1)
    scale = (1.0 / (totals[:, :, 0] * totals[:, :, 1])).reshape(16)
    serial = lax.axis_index("view") * 16 + jnp.arange(16)
    step = 1.0 + 0.29 * jnp.mod(0.6180339887 * serial.astype(F32) + 0.07, 1.0)
    step = jnp.stack([step, 1.0 / step])
    both = jnp.stack([coarse, coarse[..., ::-1]], axis=3).reshape(16, 2, 2, TAPS)

    def base(taps, size):
        gap = jnp.zeros((16, 2, size - TAPS), F32)
        return jnp.concatenate([taps[..., 4:], gap, taps[..., :4]], axis=-1)

    base_y = base(both[:, 0], 128)
    base_x = base(both[:, 1], 256)
    vmem = pl.BlockSpec(memory_space=pltpu.VMEM)
    smem = pl.BlockSpec(memory_space=pltpu.SMEM)
    hbm = pl.BlockSpec(memory_space=pl.ANY)
    volume = (8, 128, 256)
    updated, sums = pl.pallas_call(
        kernel,
        out_shape=(
            jax.ShapeDtypeStruct((8, ROWS, 256), F32),
            jax.ShapeDtypeStruct((2, 128), F32),
        ),
        in_specs=[hbm, hbm, hbm, vmem, vmem, smem, smem, smem, vmem],
        out_specs=(vmem, vmem),
        scratch_shapes=[
            pltpu.VMEM((2, 8) + volume, BF16),
            pltpu.VMEM((2,) + volume, F32),
            pltpu.VMEM((2, 1024, 256), BF16),
            pltpu.VMEM((2, 128, 1024), BF16),
            pltpu.VMEM((16, 256, 256), BF16),
            pltpu.VMEM((16, 256, 256), BF16),
            pltpu.VMEM((8, 256, 256), BF16),
            pltpu.VMEM((8,) + volume, BF16),
            pltpu.VMEM((16, 128, 256), F32),
            pltpu.VMEM((2, 16, 128, 256), F32),
            pltpu.VMEM((2, 16, 128, 256), F32),
            pltpu.VMEM(volume, F32),
            pltpu.VMEM(volume, F32),
            pltpu.VMEM(volume, F32),
            pltpu.VMEM(volume, F32),
            pltpu.VMEM((2, 8, ROWS, 256), F32),
            pltpu.VMEM((2, 8, CHUNK, 256), F32),
            pltpu.VMEM((8, ROWS, 256), F32),
            pltpu.VMEM((2, 8, 256), F32),
            pltpu.VMEM((4, 2, 8, 256), F32),
            pltpu.SemaphoreType.DMA((4,)),
            pltpu.SemaphoreType.DMA((2, 16)),
            pltpu.SemaphoreType.DMA((2, 16)),
            pltpu.SemaphoreType.DMA((3, 16)),
            pltpu.SemaphoreType.DMA((3, 16)),
            pltpu.SemaphoreType.DMA((2, 5)),
            pltpu.SemaphoreType.DMA((2, 5)),
            pltpu.SemaphoreType.DMA((4,)),
            pltpu.SemaphoreType.DMA((4,)),
        ],
        compiler_params=pltpu.CompilerParams(
            collective_id=0, has_side_effects=True, vmem_limit_bytes=60 * 1024 * 1024
        ),
        name="deconvolve",
    )(estimate, observed, voxel_weights, base_x, base_y, scale, axial, step, jnp.asarray(scale_tiles()))
    return updated, sums[:, 0] / voxel_total


def solution(mesh):
    placed = (
        P("depth", "view", None),
        P("view", "depth", None, None),
        P("view", None, "depth", None, None),
        P("view", None, None, None),
        P("view", None),
    )
    return jax.shard_map(
        body,
        mesh=mesh,
        in_specs=placed,
        out_specs=(P("depth", "view", None), P("view")),
        check_vma=False,
    )
```

time: 991 us -> 162 us (0.16)
  other arithmetic: 701 us -> 6.4 us
  waiting for transfers between devices: 161 us -> 0 us
  Pallas kernels: 0 us -> 153 us
  blocking collectives: 55.2 us -> 0 us
  starting transfers between devices: 41.1 us -> 0 us
  between operations: 14.4 us -> 0.69 us
  local copies, waits for them, and re-layouts: 14.9 us -> 2.59 us
    add x12 -> x1, other arithmetic: 368 us -> 0.02 us  [body(): step = 1.0 + 0.29 * jnp.mod(0.6180339887 * serial.astype(F32) + 0.07, 1.0)]
    reduce_sum x10 -> x2, other arithmetic: 291 us -> 1.61 us  [the longest x1 0.81 us: body(): totals = jnp.sum(coarse, axis=-1)]
    pallas_call x0 -> x1, Pallas kernels: none -> 153 us  [body(): pl.pallas_call(kernel, out_shape=(jax.ShapeDtypeStruct((8, ROWS, 256), F3...]
    reduce_scatter x2 -> x0, waiting for transfers between devices: 80.4 us -> none  [body(): lax.psum_scatter(log_terms, 'view', scatter_dimension=1, tiled=True)]
    all_gather x2 -> x0, waiting for transfers between devices: 68 us -> none  [body(): gathered = lax.all_gather(current, 'view', axis=1, tiled=True)]
    psum x1 -> x0, blocking collectives: 55.2 us -> none  [body(): divergence = lax.psum(local_sums, 'depth') / voxel_total]
    ppermute x10 -> x0, starting transfers between devices: 41 us -> none  [the longest x5 34.3 us: padded_2(): lax.ppermute(tail, axis, [(i, (i + 1) % count) for i in range(ends)])]
    mul x4 -> x0, other arithmetic: 21.5 us -> none  [the longest x2 18.3 us: lateral_adjoint(): stacked = weights.astype(jnp.float32) * values[None]]
  transfers between devices with their start and end apart: 14 -> 0, of which waited for: 10 -> 0; matrix products, arithmetic and copies ran while one was open for 2% -> 0% of each run, Pallas kernels for 0% -> 0%
where the time goes in v1:
time: 162 us
  Pallas kernels  153 us (94%)
  other arithmetic  6.4 us (4%)
  local copies, waits for them, and re-layouts  2.59 us (2%)
    pallas_call x1, Pallas kernels, body(): pl.pallas_call(kernel, out_shape=(jax.ShapeDtypeStruct((8, ROWS, 256), F3...  153 us

profile of v1, /device:TPU:0, one launch (start us, length us, event | category | flops | bytes accessed | tf_op | source)
XLA Modules:
  0.0 162.2 jit_solution(2249650168165648276)
XLA Ops:
  0.6 0.8 reduce_sum.19
  1.4 1.3 broadcast_divide_fusion.axial
  2.8 0.1 pad.3.clone
  2.9 0.6 pad_maximum_fusion.3.step
  3.4 0.1 pad.6.clone
  3.5 0.8 reduce-precision_reduce_fusion
  4.3 0.2 fusion.4
  4.5 0.6 div.31.scale
  5.1 0.1 rev.3
  5.3 0.1 slice.40
  5.4 0.7 pad_maximum_fusion.2.base_y
  6.0 0.1 slice.38
  6.1 0.7 pad_maximum_fusion.base_x
  6.8 152.5 %deconvolve.1 = (f32[8,16,256]{2,1,0:T(8,128)}, f32[2,128]{1,0:T(2,128)}) custom-call(f32[8,16,256]{2,1,0:T(8,128)} %est.1, f32[2,8,128,256]{3,2,1,0:T(8,128)} %obs.1, bf16[2,8,8,128,256]{4,3,2,1,0:T(8,128)(2,1)} %wgt.1, f32[16,2,256]{2,1,0:T(2,128)} %pad_maximum_fusion.base_x, f32[16,2,128]{2,1,0:T(2,128)} %pad_maximum_fusion.2.base_y, f32[16]{0:T(128)} %div.31.scale, ...), custom_call_target="tpu_custom_call" | custom-call | tf_op jit(solution)/shard_map/deconvolve/pallas_call | solution.py:426
  159.4 1.3 multiply_reduce_fusion
  160.6 1.6 copy.17
  (6 shorter events, 0.1 us)

commit v2 on v1

v2 whole, which is shorter than its diff:
```python
import numpy as np
import jax
import jax.numpy as jnp
from jax import lax
from jax.experimental import pallas as pl
from jax.experimental.pallas import tpu as pltpu
from jax.sharding import PartitionSpec as P

BASES = 8
TAPS = 9
RADIUS = 4
ITERS = 2
F32 = jnp.float32
BF16 = jnp.bfloat16
ROWS = 16
CHUNK = 32
HALF = 4


def spread(count, stride, reach):
    return 1.0 + reach * np.mod(stride * np.arange(count) + 0.13, 1.0)


def scale_tiles():
    rows = np.broadcast_to(spread(8, 0.5698402910, 0.37)[:, None], (8, 256))
    lanes = np.broadcast_to(spread(256, 0.7548776662, 0.41)[None, :], (8, 256))
    return np.stack([rows, 1.0 / rows, lanes, 1.0 / lanes, lanes / rows]).astype(np.float32)


def scale_steps():
    step = spread(128, 0.6180339887, 0.29)
    return np.stack([step, 1.0 / step]).astype(np.float32)


def tiled(x, tile):
    return (x.reshape(x.shape[0] // 8, 8, 256) * tile[None]).reshape(x.shape)


def kernel(
    est, obs, wgt, lateral, axial, steps, tiles,
    out, div_out,
    w, ob, tyf, tya, txf, txa, gains, coef, g, mid, mid_t, field, s_field, r_field, acc, ratio,
    log_s, log_r, far, near, zbuf, sums, peers,
    load_sem, ag_send, ag_recv, halo_send, halo_recv, rs_send, rs_recv, div_send, div_recv,
):
    vi = lax.axis_index("view")
    d = lax.axis_index("depth")
    y = vi // 2
    zl = vi % 2
    core = d % 2
    y_up = (y + 1) % 4
    y_dn = (y + 3) % 4
    v_up = y_up * 2 + zl
    v_dn = y_dn * 2 + zl
    v_z = y * 2 + 1 - zl
    v_up_z = y_up * 2 + 1 - zl
    v_dn_z = y_dn * 2 + 1 - zl
    d_up = (d + 1) % 16
    d_dn = (d + 15) % 16
    d_out = (d + 15 + 2 * core) % 16
    d_in = d + 1 - 2 * core
    partners = [d_in, d + 2 - 4 * ((d // 2) % 2), d + 4 - 8 * ((d // 4) % 2), d + 8 - 16 * (d // 8)]

    loads = [
        pltpu.make_async_copy(est, field.at[0, pl.ds(4, 8), pl.ds(pl.multiple_of(vi * ROWS, ROWS), ROWS)], load_sem.at[0]),
        pltpu.make_async_copy(wgt.at[0], w.at[0], load_sem.at[1]),
        pltpu.make_async_copy(wgt.at[1], w.at[1], load_sem.at[2]),
        pltpu.make_async_copy(obs, ob, load_sem.at[3]),
    ]
    for copy in loads:
        copy.start()

    barrier = pltpu.get_barrier_semaphore()
    greeted = [
        {"view": v_up}, {"view": v_dn}, {"view": v_z}, {"view": v_up_z}, {"view": v_dn_z},
        {"depth": d_up}, {"depth": d_dn},
        {"depth": partners[1]}, {"depth": partners[2]}, {"depth": partners[3]},
    ]
    for who in greeted:
        pl.semaphore_signal(barrier, inc=1, device_id=who, device_id_type=pl.DeviceIdType.MESH)
    pl.semaphore_wait(barrier, len(greeted))

    def remote(src, dst, send, recv, who):
        return pltpu.make_async_remote_copy(
            src_ref=src, dst_ref=dst, send_sem=send, recv_sem=recv,
            device_id=who, device_id_type=pl.DeviceIdType.MESH,
        )

    def block(it, first, count, owner):
        return field.at[it, pl.ds(first, count), pl.ds(pl.multiple_of(owner * ROWS, ROWS), ROWS)]

    hop_of = [(vi, v_z), (vi, v_up), (vi, v_dn), (vi, v_up_z), (vi, v_dn_z), (v_dn, v_up), (v_up_z, v_dn)]

    def hop(it, part, slot):
        first, count = ((4, 8), (12 * core, 4))[part]
        owner, target = hop_of[slot]
        ref = block(it, first, count, owner)
        return remote(
            ref, ref, ag_send.at[it, part * 7 + slot], ag_recv.at[it, part * 7 + slot], {"view": target}
        )

    def outer(it):
        return remote(
            block(it, 4 + 4 * core, 4, vi), block(it, 12 - 12 * core, 4, vi),
            ag_send.at[it, 14], ag_recv.at[it, 14], {"depth": d_out},
        )

    def inner(it):
        return remote(
            field.at[it, pl.ds(8 - 4 * core, 4)], field.at[it, pl.ds(12 * core, 4)],
            ag_send.at[it, 15], ag_recv.at[it, 15], {"depth": d_in},
        )

    def gather_start(it):
        outer(it).start()
        for slot in (1, 4, 0, 3, 2):
            hop(it, 0, slot).start()

    def gather_outer(it):
        outer(it).wait_recv()
        for slot in (1, 4, 0, 3, 2):
            hop(it, 1, slot).start()

    def gather_relay(it, part):
        hop(it, part, 1).wait_recv()
        hop(it, part, 5).start()
        hop(it, part, 4).wait_recv()
        hop(it, part, 6).start()

    def gather_last(it):
        for slot in (0, 2, 3, 5, 6):
            hop(it, 0, slot).wait_recv()
        inner(it).start()
        for slot in (0, 2, 3, 5, 6):
            hop(it, 1, slot).wait_recv()
        inner(it).wait_recv()
        for part in (0, 1):
            for slot in range(7):
                hop(it, part, slot).wait_send()
        outer(it).wait_send()
        inner(it).wait_send()

        @pl.when(d == 0)
        def _():
            field[it, pl.ds(0, 4)] = jnp.zeros((4, 128, 256), F32)

        @pl.when(d == 15)
        def _():
            field[it, pl.ds(12, 4)] = jnp.zeros((4, 128, 256), F32)

    order = [(y + 2) % 4, y_up, y_dn, y]

    def rows_of(c):
        return pl.ds(pl.multiple_of(order[c] * CHUNK, CHUNK), CHUNK)

    def halo(buf, turn, v, c, up):
        slot = (v * 4 + c) * 2 + up
        return remote(
            buf.at[v, pl.ds(4 + 4 * up, 4), rows_of(c)], buf.at[v, pl.ds(12 - 12 * up, 4), rows_of(c)],
            halo_send.at[turn, slot], halo_recv.at[turn, slot], {"depth": (d + 15 + 2 * up) % 16},
        )

    def wait_halo_chunk(buf, turn, c):
        for v in (0, 1):
            for up in (0, 1):
                halo(buf, turn, v, c, up).wait_recv()

        @pl.when(d == 0)
        def _():
            buf[:, pl.ds(0, 4), rows_of(c)] = jnp.zeros((2, 4, CHUNK, 256), F32)

        @pl.when(d == 15)
        def _():
            buf[:, pl.ds(12, 4), rows_of(c)] = jnp.zeros((2, 4, CHUNK, 256), F32)

    def wait_halo_sends(buf, turn):
        for v in (0, 1):
            for c in range(4):
                for up in (0, 1):
                    halo(buf, turn, v, c, up).wait_send()

    def rs_hop(it, slot):
        def cut(start, count):
            return log_r.at[:, pl.ds(pl.multiple_of(start, ROWS), count)]

        src, dst, target = [
            (cut(order[0] * CHUNK, ROWS), far.at[0], v_up),
            (cut(order[0] * CHUNK + ROWS, ROWS), far.at[1], v_dn),
            (cut(order[1] * CHUNK, CHUNK), near.at[0], v_up),
            (cut(order[2] * CHUNK, CHUNK), near.at[1], v_dn),
            (cut(v_z * ROWS, ROWS), zbuf, v_z),
        ][slot]
        return remote(src, dst, rs_send.at[it, slot], rs_recv.at[it, slot], {"view": target})

    def div_hop(step):
        return remote(sums, peers.at[step], div_send.at[step], div_recv.at[step], {"depth": partners[step]})

    def step_of(kind, v, z):
        return steps[kind, vi * 16 + v * 8 + z]

    lanes = lax.broadcasted_iota(jnp.int32, (8, 256), 1)

    def tap_row(i, axis, size, flip):
        row = jnp.zeros((8, size), F32)
        for k in range(TAPS):
            tap = lateral[i // 8, i % 8, axis, TAPS - 1 - k if flip else k]
            row = jnp.where(lanes[:, :size] == (k - RADIUS) % size, tap, row)
        return row

    def band(row, size):
        wide = jnp.broadcast_to(row[None], (size // 8, 8, size)).reshape(size, size)
        turned = pltpu.roll(wide, 0, 1, stride=1, stride_axis=0)
        diff = lax.broadcasted_iota(jnp.int32, (size, size), 1) - lax.broadcasted_iota(jnp.int32, (size, size), 0)
        return jnp.where((diff <= RADIUS) & (diff >= -RADIUS), turned, 0.0).astype(BF16)

    def build_adjoint(i, carry):
        row_x = tap_row(i, 1, 256, False)
        row_y = tap_row(i, 0, 128, True)
        txa[i] = band(row_x, 256)
        rows = pl.ds(pl.multiple_of((i % 8) * 128, 128), 128)
        tya[i // 8, :, rows] = band(row_y, 128)
        sum_x = jnp.sum(row_x.astype(BF16).astype(F32), axis=1, keepdims=True)
        sum_y = jnp.sum(row_y.astype(BF16).astype(F32), axis=1, keepdims=True)
        gains[i] = jnp.broadcast_to(1.0 / (sum_x * sum_y), (8, 256))
        return carry

    def build_forward(i, carry):
        txf[i] = band(tap_row(i, 1, 256, True), 256)
        fwd = band(tap_row(i, 0, 128, False), 128)
        rows = pl.ds(pl.multiple_of((i % 8) * 128, 128), 128)
        tyf[i // 8, rows, pl.ds(0, 128)] = fwd
        tyf[i // 8, rows, pl.ds(128, 128)] = fwd
        return carry

    def build_axial():
        for v in (0, 1):
            total = axial[v, 0]
            for k in range(1, TAPS):
                total = total + axial[v, k]
            whole = jnp.full((8, 256), total, F32)
            for k in range(TAPS):
                coef[v, k] = jnp.full((8, 256), axial[v, k], F32) / whole

    def adjoint(v, half, values, buf):
        first = 4 * half
        for b in range(BASES):
            for q in (0, 1):
                weights = w[v, b, pl.ds(first + 2 * q, 2)].reshape(256, 256)
                if values is not None:
                    weights = (weights.astype(F32) * values[pl.ds(2 * q, 2)].reshape(256, 256)).astype(BF16)
                o = jnp.dot(weights, txa[v * 8 + b], preferred_element_type=F32)
                for h in (0, 1):
                    p = 2 * q + h
                    if values is None:
                        tile = tiles[2] * gains[v * 8 + b] * step_of(0, v, first + p)
                    else:
                        tile = tiles[4] * gains[v * 8 + b]
                    mid_t[p, b] = tiled(o[h * 128 : h * 128 + 128], tile).astype(BF16)
        for p in range(HALF):
            o = jnp.dot(tya[v], mid_t[p].reshape(1024, 256), preferred_element_type=F32)
            buf[v, 4 + first + p] = tiled(o, tiles[3] * step_of(1, v, first + p))

    def forward(it, v, half):
        last = it == ITERS - 1
        first = 4 * half
        for p in range(HALF):
            z = first + p
            total = tiled(field[it, z], coef[v, 0])
            for k in range(1, TAPS):
                total = total + tiled(field[it, z + k], coef[v, k])
            high = total.astype(BF16)
            g[p, pl.ds(0, 128)] = high
            g[p, pl.ds(128, 128)] = (total - high.astype(F32)).astype(BF16)
        for p in range(HALF):
            for q in range(4):
                o = jnp.dot(tyf[v, pl.ds(q * 256, 256)], g[p], preferred_element_type=F32)
                for h in (0, 1):
                    b = 2 * q + h
                    tile = tiles[0] * gains[v * 8 + b] * step_of(0, v, first + p)
                    mid[b, p] = tiled(o[h * 128 : h * 128 + 128], tile).astype(BF16)
        for b in range(BASES):
            for q in (0, 1):
                o = jnp.dot(mid[b, pl.ds(2 * q, 2)].reshape(256, 256), txf[v * 8 + b], preferred_element_type=F32)
                o = o.reshape(2, 128, 256) * w[v, b, pl.ds(first + 2 * q, 2)].astype(F32)
                acc[pl.ds(2 * q, 2)] = o if b == 0 else acc[pl.ds(2 * q, 2)] + o
        for p in range(HALF):
            predicted = tiled(acc[p], tiles[1] * step_of(1, v, first + p))
            seen = ob[v, first + p]
            fraction = seen / predicted
            ratio[p] = tiled(fraction, tiles[0] * step_of(0, v, first + p))
            if last:
                terms = seen * jnp.log(fraction) - seen + predicted
                sums[v] += jnp.sum(terms.reshape(16, 8, 256), axis=0)

    def product(buf, rows, z):
        totals = []
        for v in (0, 1):
            total = tiled(buf[v, z + 8, rows], coef[v, 0])
            for k in range(1, TAPS):
                total = total + tiled(buf[v, z + 8 - k, rows], coef[v, k])
            totals.append(total)
        return jnp.log(totals[0] * totals[1])

    def corrections(it, c):
        rows = rows_of(c)

        def each(z, carry):
            log_r[z, rows] = product(r_field, rows, z) - log_s[z, rows]
            return carry

        lax.fori_loop(0, 8, each, 0, unroll=2)

    def sensitivity_chunk(c):
        wait_halo_chunk(s_field, 0, c)
        rows = rows_of(c)

        def each(z, carry):
            log_s[z, rows] = product(s_field, rows, z)
            return carry

        lax.fori_loop(0, 8, each, 0, unroll=2)

    def add_rows(start, count, ref):
        rows = pl.ds(pl.multiple_of(start, ROWS), count)
        log_r[:, rows] += ref[...]

    def reduce_chunks(it):
        last = it == ITERS - 1
        for c in range(4):
            if it == 0:
                sensitivity_chunk(c)
            wait_halo_chunk(r_field, 1 + it, c)
            corrections(it, c)
            if c == 0:
                rs_hop(it, 0).start()
                rs_hop(it, 1).start()
            if c == 1:
                rs_hop(it, 0).wait_recv()
                add_rows(order[1] * CHUNK, ROWS, far.at[0])
                rs_hop(it, 2).start()
            if c == 2:
                rs_hop(it, 1).wait_recv()
                add_rows(order[2] * CHUNK + ROWS, ROWS, far.at[1])
                rs_hop(it, 3).start()
            if last:
                div_hop(c).wait()
                sums[...] += peers[c]
                if c < 3:
                    div_hop(c + 1).start()
        rs_hop(it, 2).wait_recv()
        add_rows(y * CHUNK, CHUNK, near.at[0])
        rs_hop(it, 3).wait_recv()
        add_rows(y * CHUNK, CHUNK, near.at[1])
        rs_hop(it, 4).start()
        rs_hop(it, 4).wait_recv()
        rows = pl.ds(pl.multiple_of(vi * ROWS, ROWS), ROWS)
        log_total = log_r[:, rows] + zbuf[...]
        return rows, field[it, pl.ds(4, 8), rows] * jnp.exp(log_total * (1.0 / 16.0))

    def drain(it):
        for slot in range(5):
            rs_hop(it, slot).wait_send()
        wait_halo_sends(r_field, 1 + it)
        if it == 0:
            wait_halo_sends(s_field, 0)

    def sensitivity(v):
        def each(s, carry):
            half = (s + core) % 2
            adjoint(v, half, None, s_field)
            for c in range(4):
                halo(s_field, 0, v, c, half).start()
            return carry

        lax.fori_loop(0, 2, each, 0)

    def project(it):
        last = it == ITERS - 1
        if last:
            sums[...] = jnp.zeros((2, 8, 256), F32)

        def each(s, carry):
            v = s // 2
            half = (s + core) % 2
            forward(it, v, half)
            adjoint(v, half, ratio, r_field)
            for c in range(4):
                halo(r_field, 1 + it, v, c, half).start()
            return carry

        lax.fori_loop(0, 4, each, 0)

    loads[0].wait()
    gather_start(0)
    lax.fori_loop(0, 8, build_adjoint, 0)
    loads[1].wait()
    sensitivity(0)
    gather_outer(0)
    gather_relay(0, 0)
    lax.fori_loop(8, 16, build_adjoint, 0)
    loads[2].wait()
    sensitivity(1)
    gather_relay(0, 1)
    build_axial()
    lax.fori_loop(0, 16, build_forward, 0)
    loads[3].wait()
    gather_last(0)
    for it in range(ITERS):
        last = it == ITERS - 1
        project(it)
        if last:
            div_hop(0).start()
        rows, updated = reduce_chunks(it)
        if last:
            out[...] = updated
        else:
            field[1, pl.ds(4, 8), rows] = updated
            gather_start(1)
            gather_outer(1)
            gather_relay(1, 0)
            gather_relay(1, 1)
        drain(it)
        if not last:
            gather_last(1)
    for v in (0, 1):
        div_out[v] = jnp.sum(sums[v]) * (1.0 / (128 * 128 * 256))


def body(estimate, observed, voxel_weights, lateral_taps, axial_taps):
    vmem = pl.BlockSpec(memory_space=pltpu.VMEM)
    smem = pl.BlockSpec(memory_space=pltpu.SMEM)
    hbm = pl.BlockSpec(memory_space=pl.ANY)
    volume = (8, 128, 256)
    part = (HALF, 128, 256)
    return pl.pallas_call(
        kernel,
        out_shape=(
            jax.ShapeDtypeStruct((8, ROWS, 256), F32),
            jax.ShapeDtypeStruct((2,), F32),
        ),
        in_specs=[hbm, hbm, hbm, smem, smem, smem, vmem],
        out_specs=(vmem, smem),
        scratch_shapes=[
            pltpu.VMEM((2, 8) + volume, BF16),
            pltpu.VMEM((2,) + volume, F32),
            pltpu.VMEM((2, 1024, 256), BF16),
            pltpu.VMEM((2, 128, 1024), BF16),
            pltpu.VMEM((16, 256, 256), BF16),
            pltpu.VMEM((16, 256, 256), BF16),
            pltpu.VMEM((16, 8, 256), F32),
            pltpu.VMEM((2, TAPS, 8, 256), F32),
            pltpu.VMEM((HALF, 256, 256), BF16),
            pltpu.VMEM((8,) + part, BF16),
            pltpu.VMEM((HALF, 8, 128, 256), BF16),
            pltpu.VMEM((2, 16, 128, 256), F32),
            pltpu.VMEM((2, 16, 128, 256), F32),
            pltpu.VMEM((2, 16, 128, 256), F32),
            pltpu.VMEM(part, F32),
            pltpu.VMEM(part, F32),
            pltpu.VMEM(volume, F32),
            pltpu.VMEM(volume, F32),
            pltpu.VMEM((2, 8, ROWS, 256), F32),
            pltpu.VMEM((2, 8, CHUNK, 256), F32),
            pltpu.VMEM((8, ROWS, 256), F32),
            pltpu.VMEM((2, 8, 256), F32),
            pltpu.VMEM((4, 2, 8, 256), F32),
            pltpu.SemaphoreType.DMA((4,)),
            pltpu.SemaphoreType.DMA((2, 16)),
            pltpu.SemaphoreType.DMA((2, 16)),
            pltpu.SemaphoreType.DMA((3, 16)),
            pltpu.SemaphoreType.DMA((3, 16)),
            pltpu.SemaphoreType.DMA((2, 5)),
            pltpu.SemaphoreType.DMA((2, 5)),
            pltpu.SemaphoreType.DMA((4,)),
            pltpu.SemaphoreType.DMA((4,)),
        ],
        compiler_params=pltpu.CompilerParams(
            collective_id=0, has_side_effects=True, vmem_limit_bytes=60 * 1024 * 1024
        ),
        name="deconvolve",
    )(
        estimate, observed, voxel_weights, lateral_taps, axial_taps,
        jnp.asarray(scale_steps()), jnp.asarray(scale_tiles()),
    )


def solution(mesh):
    placed = (
        P("depth", "view", None),
        P("view", "depth", None, None),
        P("view", None, "depth", None, None),
        P("view", None, None, None),
        P("view", None),
    )
    return jax.shard_map(
        body,
        mesh=mesh,
        in_specs=placed,
        out_specs=(P("depth", "view", None), P("view")),
        check_vma=False,
    )
```

time: 162 us -> 140 us (0.86)
  Pallas kernels: 153 us -> 137 us
  other arithmetic: 6.4 us -> 0 us
    pallas_call x1, Pallas kernels: 153 us -> 137 us  [body(): pl.pallas_call(kernel, out_shape=(jax.ShapeDtypeStruct((8, ROWS, 256), F3...]
    div x3 -> x0, other arithmetic: 2.75 us -> none  [the longest x1 1.33 us: body(): axial = axial_taps / jnp.sum(axial_taps, axis=-1, keepdims=True)]
where the time goes in v2:
time: 140 us
  Pallas kernels  137 us (98%)
  local copies, waits for them, and re-layouts  2.74 us (2%)
    pallas_call x1, Pallas kernels, body(): pl.pallas_call(kernel, out_shape=(jax.ShapeDtypeStruct((8, ROWS, 256), F3...  137 us

profile of v2, /device:TPU:0, one launch (start us, length us, event | category | flops | bytes accessed | tf_op | source)
XLA Modules:
  0.0 140.1 jit_solution(8185837967679357400)
XLA Ops:
  0.6 136.7 %deconvolve.1 = (f32[8,16,256]{2,1,0:T(8,128)}, f32[2]{0:T(128)}) custom-call(f32[8,16,256]{2,1,0:T(8,128)} %est.1, f32[2,8,128,256]{3,2,1,0:T(8,128)} %obs.1, bf16[2,8,8,128,256]{4,3,2,1,0:T(8,128)(2,1)} %wgt.1, f32[2,8,2,9]{3,2,1,0:T(2,128)} %lateral.1, f32[2,9]{1,0:T(2,128)} %axial.1, f32[2,128]{1,0:T(2,128)} %constant.4.clone.steps, ...), custom_call_target="tpu_custom_call" | custom-call | tf_op jit(solution)/shard_map/deconvolve/pallas_call | solution.py:435
  137.4 1.6 %copy.11 = f32[8,16,256]{2,1,0:T(8,128)} copy(f32[8,16,256]{2,1,0:T(8,128)} %get-tuple-element.4) | data formatting | bytes 262144
  138.9 1.2 copy.12

commit v3 on v2

--- a/solution.py
+++ b/solution.py
@@ -67,8 +67,8 @@
         pltpu.make_async_copy(wgt.at[1], w.at[1], load_sem.at[2]),
         pltpu.make_async_copy(obs, ob, load_sem.at[3]),
     ]
-    for copy in loads:
-        copy.start()
+    loads[0].start()
+    loads[1].start()
 
     barrier = pltpu.get_barrier_semaphore()
     greeted = [
@@ -89,12 +89,17 @@
     def block(it, first, count, owner):
         return field.at[it, pl.ds(first, count), pl.ds(pl.multiple_of(owner * ROWS, ROWS), ROWS)]
 
-    hop_of = [(vi, v_z), (vi, v_up), (vi, v_dn), (vi, v_up_z), (vi, v_dn_z), (v_dn, v_up), (v_up_z, v_dn)]
+    straight = [(vi, v_z), (vi, v_up), (vi, v_dn), (v_z, v_up), (v_z, v_dn), (v_dn, v_up), (v_up_z, v_dn)]
+    diagonal = straight[:3] + [(vi, v_up_z), (vi, v_dn_z)] + straight[5:]
+
+    inner_plane = 4 - 4 * core
+    outer_plane = 4 * core
+    plane_of = [inner_plane, outer_plane]
 
     def hop(it, part, slot):
-        first, count = ((4, 8), (12 * core, 4))[part]
-        owner, target = hop_of[slot]
-        ref = block(it, first, count, owner)
+        first = (4 + inner_plane, 4 + outer_plane, 12 * core)[part]
+        owner, target = (diagonal if it == 1 and part > 0 else straight)[slot]
+        ref = block(it, first, 4, owner)
         return remote(
             ref, ref, ag_send.at[it, part * 7 + slot], ag_recv.at[it, part * 7 + slot], {"view": target}
         )
@@ -102,39 +107,40 @@
     def outer(it):
         return remote(
             block(it, 4 + 4 * core, 4, vi), block(it, 12 - 12 * core, 4, vi),
-            ag_send.at[it, 14], ag_recv.at[it, 14], {"depth": d_out},
+            ag_send.at[it, 21], ag_recv.at[it, 21], {"depth": d_out},
         )
 
     def inner(it):
         return remote(
             field.at[it, pl.ds(8 - 4 * core, 4)], field.at[it, pl.ds(12 * core, 4)],
-            ag_send.at[it, 15], ag_recv.at[it, 15], {"depth": d_in},
+            ag_send.at[it, 22], ag_recv.at[it, 22], {"depth": d_in},
         )
 
-    def gather_start(it):
-        outer(it).start()
-        for slot in (1, 4, 0, 3, 2):
-            hop(it, 0, slot).start()
-
-    def gather_outer(it):
-        outer(it).wait_recv()
-        for slot in (1, 4, 0, 3, 2):
-            hop(it, 1, slot).start()
-
-    def gather_relay(it, part):
+    def gather_own(it, part):
+        for slot in (1, 4, 0, 3, 2) if it == 1 and part > 0 else (0, 1, 2):
+            hop(it, part, slot).start()
+
+    def gather_near(it, part):
+        if not (it == 1 and part > 0):
+            hop(it, part, 0).wait_recv()
+            hop(it, part, 4).start()
+            hop(it, part, 3).start()
         hop(it, part, 1).wait_recv()
         hop(it, part, 5).start()
+
+    def gather_far(it, part):
         hop(it, part, 4).wait_recv()
         hop(it, part, 6).start()
 
+    def gather_rest(it, part):
+        for slot in (0, 2, 3, 5, 6) if it == 1 and part > 0 else (2, 3, 5, 6):
+            hop(it, part, slot).wait_recv()
+
     def gather_last(it):
-        for slot in (0, 2, 3, 5, 6):
-            hop(it, 0, slot).wait_recv()
-        inner(it).start()
-        for slot in (0, 2, 3, 5, 6):
-            hop(it, 1, slot).wait_recv()
+        for part in (1, 2):
+            gather_rest(it, part)
         inner(it).wait_recv()
-        for part in (0, 1):
+        for part in (0, 1, 2):
             for slot in range(7):
                 hop(it, part, slot).wait_send()
         outer(it).wait_send()
@@ -160,18 +166,19 @@
             halo_send.at[turn, slot], halo_recv.at[turn, slot], {"depth": (d + 15 + 2 * up) % 16},
         )
 
-    def wait_halo_chunk(buf, turn, c):
+    def wait_halo_chunk(buf, turn, phase, c):
+        up = (core, 1 - core)[phase]
         for v in (0, 1):
-            for up in (0, 1):
-                halo(buf, turn, v, c, up).wait_recv()
-
-        @pl.when(d == 0)
-        def _():
-            buf[:, pl.ds(0, 4), rows_of(c)] = jnp.zeros((2, 4, CHUNK, 256), F32)
-
-        @pl.when(d == 15)
-        def _():
-            buf[:, pl.ds(12, 4), rows_of(c)] = jnp.zeros((2, 4, CHUNK, 256), F32)
+            halo(buf, turn, v, c, up).wait_recv()
+        if phase == 1:
+
+            @pl.when(d == 0)
+            def _():
+                buf[:, pl.ds(0, 4), rows_of(c)] = jnp.zeros((2, 4, CHUNK, 256), F32)
+
+            @pl.when(d == 15)
+            def _():
+                buf[:, pl.ds(12, 4), rows_of(c)] = jnp.zeros((2, 4, CHUNK, 256), F32)
 
     def wait_halo_sends(buf, turn):
         for v in (0, 1):
@@ -179,18 +186,20 @@
                 for up in (0, 1):
                     halo(buf, turn, v, c, up).wait_send()
 
-    def rs_hop(it, slot):
+    def rs_hop(it, phase, slot):
         def cut(start, count):
-            return log_r.at[:, pl.ds(pl.multiple_of(start, ROWS), count)]
+            return log_r.at[pl.ds(plane_of[phase], 4), pl.ds(pl.multiple_of(start, ROWS), count)]
 
         src, dst, target = [
-            (cut(order[0] * CHUNK, ROWS), far.at[0], v_up),
-            (cut(order[0] * CHUNK + ROWS, ROWS), far.at[1], v_dn),
-            (cut(order[1] * CHUNK, CHUNK), near.at[0], v_up),
-            (cut(order[2] * CHUNK, CHUNK), near.at[1], v_dn),
-            (cut(v_z * ROWS, ROWS), zbuf, v_z),
+            (cut(order[0] * CHUNK, ROWS), far.at[phase, 0], v_up),
+            (cut(order[0] * CHUNK + ROWS, ROWS), far.at[phase, 1], v_dn),
+            (cut(order[1] * CHUNK, CHUNK), near.at[phase, 0], v_up),
+            (cut(order[2] * CHUNK, CHUNK), near.at[phase, 1], v_dn),
+            (cut(v_z * ROWS, ROWS), zbuf.at[phase], v_z),
         ][slot]
-        return remote(src, dst, rs_send.at[it, slot], rs_recv.at[it, slot], {"view": target})
+        return remote(
+            src, dst, rs_send.at[it, phase * 5 + slot], rs_recv.at[it, phase * 5 + slot], {"view": target}
+        )
 
     def div_hop(step):
         return remote(sums, peers.at[step], div_send.at[step], div_recv.at[step], {"depth": partners[step]})
@@ -301,78 +310,96 @@
             totals.append(total)
         return jnp.log(totals[0] * totals[1])
 
-    def corrections(it, c):
+    def corrections(it, phase, c):
         rows = rows_of(c)
 
-        def each(z, carry):
+        def each(j, carry):
+            z = plane_of[phase] + j
             log_r[z, rows] = product(r_field, rows, z) - log_s[z, rows]
             return carry
 
-        lax.fori_loop(0, 8, each, 0, unroll=2)
-
-    def sensitivity_chunk(c):
-        wait_halo_chunk(s_field, 0, c)
+        lax.fori_loop(0, 4, each, 0, unroll=2)
+
+    def sensitivity_chunk(phase, c):
         rows = rows_of(c)
 
-        def each(z, carry):
+        def each(j, carry):
+            z = plane_of[phase] + j
             log_s[z, rows] = product(s_field, rows, z)
             return carry
 
-        lax.fori_loop(0, 8, each, 0, unroll=2)
-
-    def add_rows(start, count, ref):
+        lax.fori_loop(0, 4, each, 0, unroll=2)
+
+    def add_rows(phase, start, count, ref):
         rows = pl.ds(pl.multiple_of(start, ROWS), count)
-        log_r[:, rows] += ref[...]
-
-    def reduce_chunks(it):
-        last = it == ITERS - 1
+        log_r[pl.ds(plane_of[phase], 4), rows] += ref[...]
+
+    def reduce_phase(it, phase, between):
         for c in range(4):
             if it == 0:
-                sensitivity_chunk(c)
-            wait_halo_chunk(r_field, 1 + it, c)
-            corrections(it, c)
+                wait_halo_chunk(s_field, 0, phase, c)
+                sensitivity_chunk(phase, c)
+            wait_halo_chunk(r_field, 1 + it, phase, c)
+            corrections(it, phase, c)
             if c == 0:
-                rs_hop(it, 0).start()
-                rs_hop(it, 1).start()
+                rs_hop(it, phase, 0).start()
+                rs_hop(it, phase, 1).start()
             if c == 1:
-                rs_hop(it, 0).wait_recv()
-                add_rows(order[1] * CHUNK, ROWS, far.at[0])
-                rs_hop(it, 2).start()
+                rs_hop(it, phase, 0).wait_recv()
+                add_rows(phase, order[1] * CHUNK, ROWS, far.at[phase, 0])
+                rs_hop(it, phase, 2).start()
             if c == 2:
-                rs_hop(it, 1).wait_recv()
-                add_rows(order[2] * CHUNK + ROWS, ROWS, far.at[1])
-                rs_hop(it, 3).start()
-            if last:
-                div_hop(c).wait()
-                sums[...] += peers[c]
-                if c < 3:
-                    div_hop(c + 1).start()
-        rs_hop(it, 2).wait_recv()
-        add_rows(y * CHUNK, CHUNK, near.at[0])
-        rs_hop(it, 3).wait_recv()
-        add_rows(y * CHUNK, CHUNK, near.at[1])
-        rs_hop(it, 4).start()
-        rs_hop(it, 4).wait_recv()
+                rs_hop(it, phase, 1).wait_recv()
+                add_rows(phase, order[2] * CHUNK + ROWS, ROWS, far.at[phase, 1])
+                rs_hop(it, phase, 3).start()
+            between(c)
+        rs_hop(it, phase, 2).wait_recv()
+        add_rows(phase, y * CHUNK, CHUNK, near.at[phase, 0])
+        rs_hop(it, phase, 3).wait_recv()
+        add_rows(phase, y * CHUNK, CHUNK, near.at[phase, 1])
+        rs_hop(it, phase, 4).start()
+
+    def finish(it, phase):
+        rs_hop(it, phase, 4).wait_recv()
         rows = pl.ds(pl.multiple_of(vi * ROWS, ROWS), ROWS)
-        log_total = log_r[:, rows] + zbuf[...]
-        return rows, field[it, pl.ds(4, 8), rows] * jnp.exp(log_total * (1.0 / 16.0))
+        log_total = log_r[pl.ds(plane_of[phase], 4), rows] + zbuf[phase]
+        updated = field[it, pl.ds(4 + plane_of[phase], 4), rows] * jnp.exp(log_total * (1.0 / 16.0))
+        if it == ITERS - 1:
+            out[pl.ds(plane_of[phase], 4)] = updated
+        else:
+            field[it + 1, pl.ds(4 + plane_of[phase], 4), rows] = updated
+
+    def outer_between(it):
+        def run(c):
+            if it == 0:
+                if c == 1:
+                    finish(0, 0)
+                    gather_own(1, 0)
+                if c == 3:
+                    gather_near(1, 0)
+            elif c == 0:
+                div_hop(0).start()
+            else:
+                div_hop(c - 1).wait()
+                sums[...] += peers[c - 1]
+                div_hop(c).start()
+
+        return run
 
     def drain(it):
-        for slot in range(5):
-            rs_hop(it, slot).wait_send()
+        for phase in (0, 1):
+            for slot in range(5):
+                rs_hop(it, phase, slot).wait_send()
         wait_halo_sends(r_field, 1 + it)
         if it == 0:
             wait_halo_sends(s_field, 0)
 
-    def sensitivity(v):
-        def each(s, carry):
-            half = (s + core) % 2
-            adjoint(v, half, None, s_field)
-            for c in range(4):
-                halo(s_field, 0, v, c, half).start()
-            return carry
-
-        lax.fori_loop(0, 2, each, 0)
+    def sensitivity(v, half):
+        adjoint(v, half, None, s_field)
+
+    def send_sensitivity(v, half):
+        for c in range(4):
+            halo(s_field, 0, v, c, half).start()
 
     def project(it):
         last = it == ITERS - 1
@@ -391,36 +418,64 @@
         lax.fori_loop(0, 4, each, 0)
 
     loads[0].wait()
-    gather_start(0)
+    outer(0).start()
+    gather_own(0, 1)
+    gather_own(0, 0)
     lax.fori_loop(0, 8, build_adjoint, 0)
     loads[1].wait()
-    sensitivity(0)
-    gather_outer(0)
-    gather_relay(0, 0)
+    loads[2].start()
+    loads[3].start()
+    sensitivity(0, core)
+    outer(0).wait_recv()
+    gather_own(0, 2)
+    send_sensitivity(0, core)
+    sensitivity(0, 1 - core)
+    send_sensitivity(0, 1 - core)
+    gather_near(0, 1)
+    gather_near(0, 0)
     lax.fori_loop(8, 16, build_adjoint, 0)
     loads[2].wait()
-    sensitivity(1)
-    gather_relay(0, 1)
+
+    def each_half(s, carry):
+        half = (s + core) % 2
+        sensitivity(1, half)
+        send_sensitivity(1, half)
+        return carry
+
+    lax.fori_loop(0, 2, each_half, 0)
+    gather_far(0, 1)
+    gather_far(0, 0)
+    gather_near(0, 2)
     build_axial()
     lax.fori_loop(0, 16, build_forward, 0)
     loads[3].wait()
+    gather_far(0, 2)
+    gather_rest(0, 0)
+    inner(0).start()
     gather_last(0)
     for it in range(ITERS):
-        last = it == ITERS - 1
         project(it)
-        if last:
-            div_hop(0).start()
-        rows, updated = reduce_chunks(it)
-        if last:
-            out[...] = updated
+        reduce_phase(it, 0, lambda c: None)
+        reduce_phase(it, 1, outer_between(it))
+        if it == 0:
+            gather_far(1, 0)
+            finish(0, 1)
+            outer(1).start()
+            gather_own(1, 1)
+            gather_rest(1, 0)
+            inner(1).start()
+            outer(1).wait_recv()
+            gather_own(1, 2)
+            for part in (1, 2):
+                gather_near(1, part)
+                gather_far(1, part)
         else:
-            field[1, pl.ds(4, 8), rows] = updated
-            gather_start(1)
-            gather_outer(1)
-            gather_relay(1, 0)
-            gather_relay(1, 1)
+            finish(1, 0)
+            div_hop(3).wait()
+            sums[...] += peers[3]
+            finish(1, 1)
         drain(it)
-        if not last:
+        if it == 0:
             gather_last(1)
     for v in (0, 1):
         div_out[v] = jnp.sum(sums[v]) * (1.0 / (128 * 128 * 256))
@@ -459,18 +514,18 @@
             pltpu.VMEM(part, F32),
             pltpu.VMEM(volume, F32),
             pltpu.VMEM(volume, F32),
-            pltpu.VMEM((2, 8, ROWS, 256), F32),
-            pltpu.VMEM((2, 8, CHUNK, 256), F32),
-            pltpu.VMEM((8, ROWS, 256), F32),
+            pltpu.VMEM((2, 2, 4, ROWS, 256), F32),
+            pltpu.VMEM((2, 2, 4, CHUNK, 256), F32),
+            pltpu.VMEM((2, 4, ROWS, 256), F32),
             pltpu.VMEM((2, 8, 256), F32),
             pltpu.VMEM((4, 2, 8, 256), F32),
             pltpu.SemaphoreType.DMA((4,)),
-            pltpu.SemaphoreType.DMA((2, 16)),
-            pltpu.SemaphoreType.DMA((2, 16)),
+            pltpu.SemaphoreType.DMA((2, 23)),
+            pltpu.SemaphoreType.DMA((2, 23)),
             pltpu.SemaphoreType.DMA((3, 16)),
             pltpu.SemaphoreType.DMA((3, 16)),
-            pltpu.SemaphoreType.DMA((2, 5)),
-            pltpu.SemaphoreType.DMA((2, 5)),
+            pltpu.SemaphoreType.DMA((2, 10)),
+            pltpu.SemaphoreType.DMA((2, 10)),
             pltpu.SemaphoreType.DMA((4,)),
             pltpu.SemaphoreType.DMA((4,)),
         ],

time: 140 us -> 129 us (0.921)
  Pallas kernels: 137 us -> 125 us
    pallas_call x1, Pallas kernels: 137 us -> 125 us  [body(): pl.pallas_call(kernel, out_shape=(jax.ShapeDtypeStruct((8, ROWS, 256), F3...]
where the time goes in v3:
time: 129 us
  Pallas kernels  125 us (97%)
  local copies, waits for them, and re-layouts  2.74 us (2%)
    pallas_call x1, Pallas kernels, body(): pl.pallas_call(kernel, out_shape=(jax.ShapeDtypeStruct((8, ROWS, 256), F3...  125 us
    unnamed x2, local copies, waits for them, and re-layouts  2.74 us

profile of v3, /device:TPU:0, one launch (start us, length us, event | category | flops | bytes accessed | tf_op | source)
XLA Modules:
  0.0 128.6 jit_solution(2408399719807513330)
XLA Ops:
  0.6 125.2 %deconvolve.1 = (f32[8,16,256]{2,1,0:T(8,128)}, f32[2]{0:T(128)}) custom-call(f32[8,16,256]{2,1,0:T(8,128)} %est.1, f32[2,8,128,256]{3,2,1,0:T(8,128)} %obs.1, bf16[2,8,8,128,256]{4,3,2,1,0:T(8,128)(2,1)} %wgt.1, f32[2,8,2,9]{3,2,1,0:T(2,128)} %lateral.1, f32[2,9]{1,0:T(2,128)} %axial.1, f32[2,128]{1,0:T(2,128)} %constant.4.clone.steps, ...), custom_call_target="tpu_custom_call" | custom-call | tf_op jit(solution)/shard_map/deconvolve/pallas_call | solution.py:490
  125.8 1.6 %copy.11 = f32[8,16,256]{2,1,0:T(8,128)} copy(f32[8,16,256]{2,1,0:T(8,128)} %get-tuple-element.4) | data formatting | bytes 262144
  127.4 1.2 copy.12

commit v4 on v3

--- a/solution.py
+++ b/solution.py
@@ -63,12 +63,13 @@
 
     loads = [
         pltpu.make_async_copy(est, field.at[0, pl.ds(4, 8), pl.ds(pl.multiple_of(vi * ROWS, ROWS), ROWS)], load_sem.at[0]),
-        pltpu.make_async_copy(wgt.at[0], w.at[0], load_sem.at[1]),
+        pltpu.make_async_copy(wgt.at[0, :, pl.ds(4 * core, 4)], w.at[0, :, pl.ds(4 * core, 4)], load_sem.at[1]),
         pltpu.make_async_copy(wgt.at[1], w.at[1], load_sem.at[2]),
         pltpu.make_async_copy(obs, ob, load_sem.at[3]),
+        pltpu.make_async_copy(wgt.at[0, :, pl.ds(4 - 4 * core, 4)], w.at[0, :, pl.ds(4 - 4 * core, 4)], load_sem.at[4]),
     ]
-    loads[0].start()
-    loads[1].start()
+    for which in (0, 1, 4):
+        loads[which].start()
 
     barrier = pltpu.get_barrier_semaphore()
     greeted = [
@@ -78,7 +79,6 @@
     ]
     for who in greeted:
         pl.semaphore_signal(barrier, inc=1, device_id=who, device_id_type=pl.DeviceIdType.MESH)
-    pl.semaphore_wait(barrier, len(greeted))
 
     def remote(src, dst, send, recv, who):
         return pltpu.make_async_remote_copy(
@@ -417,11 +417,12 @@
 
         lax.fori_loop(0, 4, each, 0)
 
+    lax.fori_loop(0, 8, build_adjoint, 0)
     loads[0].wait()
+    pl.semaphore_wait(barrier, len(greeted))
     outer(0).start()
     gather_own(0, 1)
     gather_own(0, 0)
-    lax.fori_loop(0, 8, build_adjoint, 0)
     loads[1].wait()
     loads[2].start()
     loads[3].start()
@@ -429,6 +430,7 @@
     outer(0).wait_recv()
     gather_own(0, 2)
     send_sensitivity(0, core)
+    loads[4].wait()
     sensitivity(0, 1 - core)
     send_sensitivity(0, 1 - core)
     gather_near(0, 1)
@@ -519,7 +521,7 @@
             pltpu.VMEM((2, 4, ROWS, 256), F32),
             pltpu.VMEM((2, 8, 256), F32),
             pltpu.VMEM((4, 2, 8, 256), F32),
-            pltpu.SemaphoreType.DMA((4,)),
+            pltpu.SemaphoreType.DMA((5,)),
             pltpu.SemaphoreType.DMA((2, 23)),
             pltpu.SemaphoreType.DMA((2, 23)),
             pltpu.SemaphoreType.DMA((3, 16)),

time: 129 us -> 129 us (level)
  no operation moved by 1% of the time
where the time goes in v4:
time: 129 us
  Pallas kernels  125 us (97%)
  local copies, waits for them, and re-layouts  2.74 us (2%)
    pallas_call x1, Pallas kernels, body(): pl.pallas_call(kernel, out_shape=(jax.ShapeDtypeStruct((8, ROWS, 256), F3...  125 us
    unnamed x2, local copies, waits for them, and re-layouts  2.74 us

profile of v4, /device:TPU:0, one launch (start us, length us, event | category | flops | bytes accessed | tf_op | source)
XLA Modules:
  0.0 128.6 jit_solution(11899356078793906414)
XLA Ops:
  0.6 125.2 %deconvolve.1 = (f32[8,16,256]{2,1,0:T(8,128)}, f32[2]{0:T(128)}) custom-call(f32[8,16,256]{2,1,0:T(8,128)} %est.1, f32[2,8,128,256]{3,2,1,0:T(8,128)} %obs.1, bf16[2,8,8,128,256]{4,3,2,1,0:T(8,128)(2,1)} %wgt.1, f32[2,8,2,9]{3,2,1,0:T(2,128)} %lateral.1, f32[2,9]{1,0:T(2,128)} %axial.1, f32[2,128]{1,0:T(2,128)} %constant.4.clone.steps, ...), custom_call_target="tpu_custom_call" | custom-call | tf_op jit(solution)/shard_map/deconvolve/pallas_call | solution.py:492
  125.8 1.6 %copy.11 = f32[8,16,256]{2,1,0:T(8,128)} copy(f32[8,16,256]{2,1,0:T(8,128)} %get-tuple-element.4) | data formatting | bytes 262144
  127.4 1.2 copy.12
